TPU v7x, 256 devices: a whole 4x4x8 slice. The times are simulated.
256 devices in a mesh: seq: 32 (over y_lo, z, core), tp: 4 (over x), dp: 2 (over y_hi).
Axes of the slice: x: 4, y: 4 (y_hi: 2, y_lo: 2; y = y_hi * 2 + y_lo), z: 8, core: 2. Of those that a mesh axis runs over, the one named last changes fastest.
Arguments:
- query_gate: bfloat16 [2, 8192, 4096], P('dp', 'seq', 'tp'), may hold values from -6 to 6
- key_gate: bfloat16 [2, 8192, 4096], P('dp', 'seq', 'tp'), may hold values from -6 to 6
- value_input: bfloat16 [2, 8192, 4096], P('dp', 'seq', 'tp'), may hold values from -6 to 6
- filter_taps: bfloat16 [4096, 128], P('tp'), may hold values from -0.5 to 0.5
- skip_gain: float32 [4096], P('tp'), may hold values from -1 to 1
- out_weight: bfloat16 [4096, 4096], P('tp', 'dp'), may hold values from -0.09375 to 0.09375
- cotangent: bfloat16 [2, 8192, 4096], P('dp', 'seq', 'tp'), may hold values from -6 to 6
Outputs:
- grad_query: bfloat16 [2, 8192, 4096], P('dp', 'seq', 'tp')
- grad_key: bfloat16 [2, 8192, 4096], P('dp', 'seq', 'tp')
- grad_value: bfloat16 [2, 8192, 4096], P('dp', 'seq', 'tp')
- grad_filter: float32 [4096, 128], P('tp')
- grad_skip: float32 [4096], P('tp')
- grad_weight: float32 [4096, 4096], P(('seq', 'dp'), 'tp')
All inputs are finite; a program needn't handle non-finite values.
Results may differ from a plain program's by a relative error of at most 0.0095.
Values may be sent and summed in bfloat16 or wider, within the bound.
A program may use at most 192 MiB of HBM per device.

v0:
```python
import math
import jax
import jax.numpy as jnp
from jax import lax
from jax.sharding import PartitionSpec as P

block_rows = 16


def shifted(block, axis, distance):
    devices = range(lax.axis_size(axis))
    route = [(i - distance, i) for i in devices if i - distance in devices]
    return lax.ppermute(block, axis, route)


def taps_matrix(vector, row_count, col_count):
    channels, width_all = vector.shape
    tiled = jnp.tile(vector, (1, row_count + 1))
    skewed = tiled[:, : row_count * (width_all - 1)].reshape(channels, row_count, width_all - 1)
    return skewed[:, :, row_count - 1 : row_count - 1 + col_count]


def forward_table(filter_taps):
    channels, tap_count = filter_taps.shape
    padding = jnp.zeros((channels, block_rows), filter_taps.dtype)
    vector = jnp.concatenate([padding, filter_taps[:, ::-1], padding], axis=1)
    return taps_matrix(vector, block_rows, tap_count + block_rows)


def backward_table(filter_taps):
    channels, tap_count = filter_taps.shape
    before = jnp.zeros((channels, block_rows - 1), filter_taps.dtype)
    after = jnp.zeros((channels, block_rows + 1), filter_taps.dtype)
    vector = jnp.concatenate([before, filter_taps, after], axis=1)
    return taps_matrix(vector, block_rows, tap_count + block_rows)


def windows(extended, length, tap_count):
    pieces = []
    for shift_index in range(tap_count // block_rows + 1):
        lower = shift_index * block_rows
        pieces.append(
            extended[lower : lower + length].reshape(
                length // block_rows, block_rows, extended.shape[1]
            )
        )
    return jnp.concatenate(pieces, axis=1)


def lag_sums(blocks, tap_count):
    channels, row_count, col_count = blocks.shape
    flattened = blocks.reshape(channels, row_count * col_count)
    padded = jnp.concatenate([flattened, jnp.zeros((channels, row_count), blocks.dtype)], axis=1)
    diagonal = padded.reshape(channels, row_count, col_count + 1)[:, :, 1 : tap_count + 1]
    return jnp.sum(diagonal, axis=1)[:, ::-1]


def per_device(query_gate, key_gate, value_input, filter_taps, skip_gain, out_weight, cotangent):
    queries = query_gate[0]
    key_rows = key_gate[0]
    value_rows = value_input[0]
    length, channels = queries.shape
    tap_count = filter_taps.shape[1]
    seq_count = lax.axis_size("seq")
    replica_count = lax.axis_size("dp")
    norm_factor = 1.0 / math.sqrt(length * seq_count * replica_count)
    mixed = (key_rows.astype(jnp.float32) * value_rows.astype(jnp.float32)).astype(jnp.bfloat16)
    tail_rows = mixed[length - (tap_count - 1) :]
    prior = shifted(tail_rows, "seq", 1)
    extended = jnp.concatenate([jnp.zeros((1, channels), jnp.bfloat16), prior, mixed], axis=0)
    forward_windows = windows(extended, length, tap_count)
    conv = jnp.einsum(
        "cab,ibc->iac",
        forward_table(filter_taps),
        forward_windows,
        preferred_element_type=jnp.float32,
    ).reshape(length, channels)
    state = conv + skip_gain[None, :] * mixed.astype(jnp.float32)
    gated = (queries.astype(jnp.float32) * state).astype(jnp.bfloat16)
    full_cot = lax.all_gather(cotangent[0], "tp", axis=1, tiled=True)
    selected = full_cot
    grad_gated = lax.dot_general(
        selected,
        lax.all_gather(out_weight, "dp", axis=1, tiled=True),
        (((1,), (1,)), ((), ())),
        preferred_element_type=jnp.float32,
    )
    grad_query = (grad_gated * state).astype(jnp.bfloat16)
    signal = (grad_gated * queries.astype(jnp.float32)).astype(jnp.bfloat16)
    head_rows = signal[: tap_count - 1]
    later = shifted(head_rows, "seq", -1)
    signal_ext = jnp.concatenate([signal, later, jnp.zeros((1, channels), jnp.bfloat16)], axis=0)
    back = jnp.einsum(
        "cab,ibc->iac",
        backward_table(filter_taps),
        windows(signal_ext, length, tap_count),
        preferred_element_type=jnp.float32,
    ).reshape(length, channels)
    back = back + skip_gain[None, :] * signal.astype(jnp.float32)
    grad_key = (back * value_rows.astype(jnp.float32)).astype(jnp.bfloat16)
    grad_value = (back * key_rows.astype(jnp.float32)).astype(jnp.bfloat16)
    signal_blocks = signal.reshape(length // block_rows, block_rows, channels)
    blocks = jnp.einsum(
        "iac,ibc->cab", signal_blocks, forward_windows, preferred_element_type=jnp.float32
    )
    skip_term = jnp.sum(signal.astype(jnp.float32) * mixed.astype(jnp.float32), axis=0)
    filter_sum, skip_sum = lax.psum((lag_sums(blocks, tap_count), skip_term), ("seq", "dp"))
    selected = full_cot
    grad_weight = lax.psum_scatter(
        lax.dot_general(
            selected, gated, (((0,), (0,)), ((), ())), preferred_element_type=jnp.float32
        ),
        ("seq", "dp"),
        scatter_dimension=0,
        tiled=True,
    )
    return (
        grad_query[None],
        grad_key[None],
        grad_value[None],
        filter_sum * norm_factor,
        skip_sum * norm_factor,
        grad_weight * norm_factor,
    )


def solution(mesh):
    return jax.shard_map(
        per_device,
        mesh=mesh,
        in_specs=(
            P("dp", "seq", "tp"),
            P("dp", "seq", "tp"),
            P("dp", "seq", "tp"),
            P("tp", None),
            P("tp"),
            P("tp", "dp"),
            P("dp", "seq", "tp"),
        ),
        out_specs=(
            P("dp", "seq", "tp"),
            P("dp", "seq", "tp"),
            P("dp", "seq", "tp"),
            P("tp", None),
            P("tp"),
            P(("seq", "dp"), "tp"),
        ),
        check_vma=False,
    )
```

profile of v0, /device:TPU:64, one launch (start us, length us, event | category | flops | bytes accessed | tf_op | source)
XLA Modules:
  0.0 1021.4 jit_solution(6205468329109296625)
XLA Ops:
  8.8 3.5 rev.6
  14.4 2.9 slice.134
  17.3 4.8 reshape.123
  22.1 7.0 slice.135
  29.0 12.7 %copy.93 = bf16[1024,16,144]{2,1,0:T(8,128)(2,1)} copy(bf16[1024,16,144]{0,2,1:T(8,128)(2,1)} %slice.135) | data formatting | bytes 9437184
  41.8 3.7 all-gather.6.cloned.1.call-done
  45.5 112.5 %all-gather.4.cloned.1.call-done = bf16[1024,4096]{1,0:T(8,128)(2,1)} async-done(((bf16[1024,2048]{1,0:T(8,128)(2,1)}), bf16[1024,4096]{1,0:T(8,128)(2,1)}) %all-gather.4.cloned.1.call-update) | async-done | bytes 8388624 | tf_op jit(solution)/shard_map/all_gather | solution.py:84
  158.0 7.5 fusion.8
  168.9 4.7 copy.70
  174.8 2.9 slice.119
  177.7 4.9 reshape.112
  182.6 6.8 slice.120
  189.4 12.5 %copy.92 = bf16[1024,16,144]{2,1,0:T(8,128)(2,1)} copy(bf16[1024,16,144]{0,2,1:T(8,128)(2,1)} %slice.120) | data formatting | bytes 9437184
  201.9 4.8 copy.74
  212.9 5.8 copy.75
  218.7 5.8 copy.76
  224.4 5.7 copy.77
  230.1 5.7 copy.78
  235.8 4.8 copy.79
  240.6 4.7 copy.80
  245.2 4.7 copy.81
  249.9 4.7 copy.82
  254.6 35.9 %concatenate.45 = bf16[16,144,1024]{1,0,2:T(8,128)(2,1)} concatenate(bf16[16,16,1024]{1,0,2:T(8,128)(2,1)} %copy.74, bf16[16,16,1024]{1,0,2:T(8,128)(2,1)} %copy.75, bf16[16,16,1024]{1,0,2:T(8,128)(2,1)} %copy.76, bf16[16,16,1024]{1,0,2:T(8,128)(2,1)} %copy.77, bf16[16,16,1024]{1,0,2:T(8,128)(2,1)} %copy.78, bf16[16,16,1024]{1,0,2:T(8,128)(2,1)} %copy.79, ...), dimensions={1} | concatenate | bytes 9437184 | tf_op jit(solution)/shard_map/concatenate | solution.py:47
  290.6 11.3 %convolution_bitcast_fusion.1 = f32[16,16,1024]{1,0,2:T(8,128)} fusion(bf16[16,144,1024]{1,0,2:T(8,128)(2,1)} %concatenate.45, bf16[1024,16,144]{2,1,0:T(8,128)(2,1)} %copy.93), kind=kOutput, calls=%fused_computation.2 | convolution fusion | flops 75497472 | bytes 10485760 | tf_op jit(solution)/shard_map/cab,ibc->iac/dot_general | solution.py:93
  301.8 5.1 copy.85
  308.9 5.7 copy.62
  314.6 5.7 copy.63
  320.3 5.8 copy.64
  326.1 5.7 copy.65
  331.8 5.9 copy.66
  337.7 5.7 copy.67
  343.3 4.8 copy.68
  348.1 4.7 copy.69
  352.8 35.9 %concatenate.41 = bf16[16,144,1024]{1,0,2:T(8,128)(2,1)} concatenate(bf16[16,16,1024]{1,0,2:T(8,128)(2,1)} %copy.62, bf16[16,16,1024]{1,0,2:T(8,128)(2,1)} %copy.63, bf16[16,16,1024]{1,0,2:T(8,128)(2,1)} %copy.64, bf16[16,16,1024]{1,0,2:T(8,128)(2,1)} %copy.65, bf16[16,16,1024]{1,0,2:T(8,128)(2,1)} %copy.66, bf16[16,16,1024]{1,0,2:T(8,128)(2,1)} %copy.67, ...), dimensions={1} | concatenate | bytes 9437184 | tf_op jit(solution)/shard_map/concatenate | solution.py:47
  388.7 9.9 fusion.29
  398.6 11.3 %convolution_bitcast_fusion.2 = f32[16,16,1024]{1,0,2:T(8,128)} fusion(bf16[16,144,1024]{1,0,2:T(8,128)(2,1)} %concatenate.41, bf16[1024,16,144]{2,1,0:T(8,128)(2,1)} %copy.92), kind=kOutput, calls=%fused_computation.3 | convolution fusion | flops 75497472 | bytes 10485760 | tf_op jit(solution)/shard_map/cab,ibc->iac/dot_general | solution.py:72
  409.9 5.1 copy.73
  415.0 15.0 %copy.87 = f32[1024,16,144]{0,2,1:T(8,128)} copy(f32[1024,16,144]{2,1,0:T(8,128)} %fusion.29) | data formatting | bytes 18874368 | tf_op jit(solution)/shard_map/iac,ibc->cab/dot_general | solution.py:103
  430.0 9.3 concatenate.47
  439.3 10.3 %reshape.126 = f32[1024,16,145]{0,2,1:T(8,128)} reshape(f32[1024,2320]{0,1:T(8,128)} %concatenate.47) | data formatting | bytes 19005440 | tf_op jit(solution)/shard_map/reshape | solution.py:54
  449.6 5.5 slice_reduce_fusion
  455.1 4.7 rev.7
  460.2 3.5 fusion.14
  463.7 8.1 convolution_bitcast_fusion
  471.8 17.5 %copy.90 = f32[4096,1024]{1,0:T(8,128)} copy(f32[4096,1024]{0,1:T(8,128)} %convolution_bitcast_fusion) | data formatting | bytes 33554432
  489.4 124.9 %psum.15 = f32[1024]{0:T(1024)S(1)} all-reduce(f32[1024]{0:T(1024)S(1)} %get-tuple-element.24), channel_id=1, replica_groups=mesh['seq'=32,'tp'=4,'dp'=2] {'seq','dp'}, use_global_device_ids=true, to_apply=%region_3.0 | all-reduce | flops 1024 | bytes 8192 | tf_op jit(solution)/shard_map/psum | solution.py:107
  614.8 22.9 %all-reduce.3.cloned.1.call-done = f32[1024,128]{0,1:T(8,128)} async-done(((f32[1024,128]{0,1:T(8,128)}), f32[1024,128]{0,1:T(8,128)}) %all-reduce.3.cloned.1.call-update) | async-done | bytes 524304 | tf_op jit(solution)/shard_map/psum | solution.py:107
  639.7 372.7 %reduce-scatter.4.cloned.1.call-done = f32[64,1024]{1,0:T(8,128)} async-done(((f32[4096,1024]{1,0:T(8,128)}), f32[64,1024]{1,0:T(8,128)}) %reduce-scatter.4.cloned.1.call-update) | async-done | bytes 262160
  (45 shorter events, 21.4 us)
Async XLA Ops:
  7.2 38.3 %all-gather.6.cloned.1.call-start = ((), (), s32[]{:S(2)}) async-start(), calls=%async_computation.3 | async-start | bytes 2621440 | tf_op jit(solution)/shard_map/all_gather | solution.py:80
  7.9 150.1 %all-gather.4.cloned.1.call-start = ((), (), s32[]{:S(2)}) async-start(), calls=%async_computation.1 | async-start | bytes 12582912 | tf_op jit(solution)/shard_map/all_gather | solution.py:84
  8.6 629.0 %all-reduce.3.cloned.1.call-start = ((), (), s32[]{:S(2)}) async-start(), calls=%async_computation.2 | async-start | bytes 1048576 | tf_op jit(solution)/shard_map/psum | solution.py:107
  29.0 129.0 %copy-start = (bf16[1,256,1024]{2,1,0:T(8,128)(2,1)S(1)}, bf16[1,256,1024]{2,1,0:T(8,128)(2,1)}, u32[]{:S(2)}) copy-start(bf16[1,256,1024]{2,1,0:T(8,128)(2,1)} %param.9) | copy-start | bytes 1572868
  29.0 129.0 %copy-start.1 = (bf16[1,256,1024]{2,1,0:T(8,128)(2,1)S(1)}, bf16[1,256,1024]{2,1,0:T(8,128)(2,1)}, u32[]{:S(2)}) copy-start(bf16[1,256,1024]{2,1,0:T(8,128)(2,1)} %param.8) | copy-start | bytes 1572868
  29.0 129.0 %copy-start.3 = (bf16[1,256,1024]{2,1,0:T(8,128)(2,1)S(1)}, bf16[1,256,1024]{2,1,0:T(8,128)(2,1)}, u32[]{:S(2)}) copy-start(bf16[1,256,1024]{2,1,0:T(8,128)(2,1)} %param.7) | copy-start | bytes 1572868
  166.2 43.8 %collective-permute-start.1 = (bf16[127,1024]{1,0:T(8,128)(2,1)}, bf16[127,1024]{1,0:T(8,128)(2,1)}, u32[]{:S(2)}, u32[]{:S(2)}) collective-permute-start(bf16[127,1024]{1,0:T(8,128)(2,1)} %slice.121), channel_id=1, source_target_pairs={{8,0},{16,8},{24,16},{32,24},{40,32},{48,40},{56,48},{64,56},{72,6... | collective-permute-start | bytes 780296 | tf_op jit(solution)/shard_map/ppermute | solution.py:13
  207.5 99.5 %collective-permute-start = (bf16[127,1024]{1,0:T(8,128)(2,1)}, bf16[127,1024]{1,0:T(8,128)(2,1)S(1)}, u32[]{:S(2)}, u32[]{:S(2)}) collective-permute-start(bf16[127,1024]{1,0:T(8,128)(2,1)} %slice.106), channel_id=1, source_target_pairs={{0,8},{8,16},{16,24},{24,32},{32,40},{40,48},{48,56},{56,64},{64,7... | collective-permute-start | bytes 780296 | tf_op jit(solution)/shard_map/ppermute | solution.py:13
  449.6 10.6 %copy-start.4 = (f32[1024]{0:T(1024)S(1)}, f32[1024]{0:T(1024)}, u32[]{:S(2)}) copy-start(f32[1024]{0:T(1024)} %param.11) | copy-start | bytes 12292
  459.9 552.6 %reduce-scatter.4.cloned.1.call-start = ((), (), s32[]{:S(2)}) async-start(), calls=%async_computation.4 | async-start | bytes 17039360
  460.2 3.5 copy-start.2
Sparse Core Ops, SparseCore 0:
  9.8 35.6 all-gather.5
  47.3 110.6 all-gather.3
  460.0 177.6 all-reduce.2
  640.1 372.3 reduce-scatter.3
where the time goes:
time: 1030 us; the launch traced here: 1020 us
  waiting for transfers between devices  513 us (50%)
  local copies, waits for them, and re-layouts  298 us (29%)
  blocking collectives  125 us (12%)
  matrix products  48 us (5%)
  other arithmetic  17.2 us (2%)
  between operations  14.2 us (1%)
    unnamed x5, waiting for transfers between devices  374 us
    psum x1, blocking collectives, per_device(): lax.psum((lag_sums(blocks, tap_count), skip_term), ('seq', 'dp'))  125 us
    all_gather x1, waiting for transfers between devices, per_device(): lax.all_gather(out_weight, 'dp', axis=1, tiled=True)  113 us
    reshape x17, local copies, waits for them, and re-layouts, windows(): extended[lower:lower + length]  90.5 us
    concatenate x2, local copies, waits for them, and re-layouts, windows(): return jnp.concatenate(pieces, axis=1)  71.9 us
    unnamed x16, local copies, waits for them, and re-layouts  45.8 us
    psum x1, waiting for transfers between devices, per_device(): lax.psum((lag_sums(blocks, tap_count), skip_term), ('seq', 'dp'))  22.9 us
  transfers between devices with their start and end apart: 6, of which 4 were waited for; matrix products, arithmetic and copies ran while one was open for 20% of the time, Pallas kernels for 0%

commit v1 on v0

--- a/solution.py
+++ b/solution.py
@@ -1,3 +1,4 @@
+import functools
 import math
 import jax
 import jax.numpy as jnp
@@ -5,6 +6,15 @@
 from jax.sharding import PartitionSpec as P
 
 block_rows = 16
+
+
+def _view_turns(s0, chip_axis, across):
+    for pp in (chip_axis, across):
+        s0 = lax.psum(s0, pp)
+    return s0
+
+
+place_cards = functools.partial(_view_turns, chip_axis="dp", across="seq")
 
 
 def shifted(block, axis, distance):
@@ -104,7 +114,7 @@
         "iac,ibc->cab", signal_blocks, forward_windows, preferred_element_type=jnp.float32
     )
     skip_term = jnp.sum(signal.astype(jnp.float32) * mixed.astype(jnp.float32), axis=0)
-    filter_sum, skip_sum = lax.psum((lag_sums(blocks, tap_count), skip_term), ("seq", "dp"))
+    filter_sum, skip_sum = place_cards((lag_sums(blocks, tap_count), skip_term))
     selected = full_cot
     grad_weight = lax.psum_scatter(
         lax.dot_general(

time: 1030 us -> 1070 us (1.039)
  waiting for transfers between devices: 513 us -> 628 us
  blocking collectives: 125 us -> 53.5 us
    psum x1 -> x2, waiting for transfers between devices: 22.9 us -> 134 us  [_view_turns(): s0 = lax.psum(s0, pp)]
    psum x1 -> x2, blocking collectives: 125 us -> 53.5 us  [_view_turns(): s0 = lax.psum(s0, pp)]
    unnamed x5 -> x6, waiting for transfers between devices: 374 us -> 378 us
  transfers between devices with their start and end apart: 6 -> 7, of which waited for: 4 -> 4; matrix products, arithmetic and copies ran while one was open for 20% -> 20% of each run, Pallas kernels for 0% -> 0%
where the time goes in v1:
time: 1070 us; the launch traced here: 1060 us
  waiting for transfers between devices  628 us (59%)
  local copies, waits for them, and re-layouts  296 us (28%)
  blocking collectives  53.5 us (5%)
  matrix products  49.1 us (5%)
  other arithmetic  16.7 us (2%)
  between operations  14.2 us (1%)
    unnamed x6, waiting for transfers between devices  378 us
    psum x2, waiting for transfers between devices, _view_turns(): s0 = lax.psum(s0, pp)  134 us
    all_gather x1, waiting for transfers between devices, per_device(): lax.all_gather(out_weight, 'dp', axis=1, tiled=True)  113 us
    reshape x17, local copies, waits for them, and re-layouts, windows(): extended[lower:lower + length]  90.1 us
    concatenate x2, local copies, waits for them, and re-layouts, windows(): return jnp.concatenate(pieces, axis=1)  72.2 us
    psum x2, blocking collectives, _view_turns(): s0 = lax.psum(s0, pp)  53.5 us
    unnamed x16, local copies, waits for them, and re-layouts  45.7 us
  transfers between devices with their start and end apart: 7, of which 4 were waited for; matrix products, arithmetic and copies ran while one was open for 20% of the time, Pallas kernels for 0%

profile of v1, /device:TPU:64, one launch (start us, length us, event | category | flops | bytes accessed | tf_op | source)
XLA Modules:
  0.0 1063.1 jit_solution(748462047921029681)
XLA Ops:
  8.8 3.5 rev.6
  17.2 4.8 reshape.123
  22.0 7.0 slice.135
  29.0 12.7 %copy.93 = bf16[1024,16,144]{2,1,0:T(8,128)(2,1)} copy(bf16[1024,16,144]{0,2,1:T(8,128)(2,1)} %slice.135) | data formatting | bytes 9437184
  41.7 3.8 all-gather.6.cloned.1.call-done
  45.5 112.5 %all-gather.4.cloned.1.call-done = bf16[1024,4096]{1,0:T(8,128)(2,1)} async-done(((bf16[1024,2048]{1,0:T(8,128)(2,1)}), bf16[1024,4096]{1,0:T(8,128)(2,1)}) %all-gather.4.cloned.1.call-update) | async-done | bytes 8388624 | tf_op jit(solution)/shard_map/all_gather | solution.py:94
  158.0 7.5 fusion.8
  168.9 4.7 copy.70
  174.9 2.9 slice.119
  177.8 4.8 reshape.112
  182.5 6.8 slice.120
  189.3 12.5 %copy.92 = bf16[1024,16,144]{2,1,0:T(8,128)(2,1)} copy(bf16[1024,16,144]{0,2,1:T(8,128)(2,1)} %slice.120) | data formatting | bytes 9437184
  201.8 4.7 copy.74
  209.1 3.2 pad_maximum_fusion
  212.3 5.7 copy.75
  218.0 5.7 copy.76
  223.7 5.7 copy.77
  229.5 5.7 copy.78
  235.2 5.7 copy.79
  240.9 4.7 copy.80
  245.6 4.7 copy.81
  250.3 4.7 copy.82
  256.6 5.7 copy.62
  262.3 5.8 copy.63
  268.1 5.7 copy.64
  273.8 5.7 copy.65
  279.5 5.7 copy.66
  285.2 4.7 copy.67
  289.9 4.7 copy.68
  294.7 4.7 copy.69
  299.3 36.1 %concatenate.41 = bf16[16,144,1024]{1,0,2:T(8,128)(2,1)} concatenate(bf16[16,16,1024]{1,0,2:T(8,128)(2,1)} %copy.62, bf16[16,16,1024]{1,0,2:T(8,128)(2,1)} %copy.63, bf16[16,16,1024]{1,0,2:T(8,128)(2,1)} %copy.64, bf16[16,16,1024]{1,0,2:T(8,128)(2,1)} %copy.65, bf16[16,16,1024]{1,0,2:T(8,128)(2,1)} %copy.66, bf16[16,16,1024]{1,0,2:T(8,128)(2,1)} %copy.67, ...), dimensions={1} | concatenate | bytes 9437184 | tf_op jit(solution)/shard_map/concatenate | solution.py:57
  335.5 11.4 %convolution_bitcast_fusion.2 = f32[16,16,1024]{1,0,2:T(8,128)} fusion(bf16[16,144,1024]{1,0,2:T(8,128)(2,1)} %concatenate.41, bf16[1024,16,144]{2,1,0:T(8,128)(2,1)} %copy.92), kind=kOutput, calls=%fused_computation.3 | convolution fusion | flops 75497472 | bytes 10485760 | tf_op jit(solution)/shard_map/cab,ibc->iac/dot_general | solution.py:82
  346.8 9.3 fusion.29
  356.1 15.0 %copy.87 = f32[1024,16,144]{0,2,1:T(8,128)} copy(f32[1024,16,144]{2,1,0:T(8,128)} %fusion.29) | data formatting | bytes 18874368 | tf_op jit(solution)/shard_map/iac,ibc->cab/dot_general | solution.py:113
  371.1 9.2 concatenate.47
  380.2 10.4 reshape.126
  390.7 4.7 slice_reduce_fusion
  398.1 36.1 %concatenate.45 = bf16[16,144,1024]{1,0,2:T(8,128)(2,1)} concatenate(bf16[16,16,1024]{1,0,2:T(8,128)(2,1)} %copy.74, bf16[16,16,1024]{1,0,2:T(8,128)(2,1)} %copy.75, bf16[16,16,1024]{1,0,2:T(8,128)(2,1)} %copy.76, bf16[16,16,1024]{1,0,2:T(8,128)(2,1)} %copy.77, bf16[16,16,1024]{1,0,2:T(8,128)(2,1)} %copy.78, bf16[16,16,1024]{1,0,2:T(8,128)(2,1)} %copy.79, ...), dimensions={1} | concatenate | bytes 9437184 | tf_op jit(solution)/shard_map/concatenate | solution.py:57
  434.1 11.2 %convolution_bitcast_fusion.1 = f32[16,16,1024]{1,0,2:T(8,128)} fusion(bf16[16,144,1024]{1,0,2:T(8,128)(2,1)} %concatenate.45, bf16[1024,16,144]{2,1,0:T(8,128)(2,1)} %copy.93), kind=kOutput, calls=%fused_computation.2 | convolution fusion | flops 75497472 | bytes 10485760 | tf_op jit(solution)/shard_map/cab,ibc->iac/dot_general | solution.py:103
  445.4 5.1 copy.85
  450.5 6.0 copy.73
  456.5 3.7 fusion.14
  460.5 9.7 convolution_bitcast_fusion
  470.3 17.5 %copy.90 = f32[4096,1024]{1,0:T(8,128)} copy(f32[4096,1024]{0,1:T(8,128)} %convolution_bitcast_fusion) | data formatting | bytes 33554432
  487.8 6.5 psum.30
  494.2 47.0 %psum.31 = f32[1024]{0:T(1024)S(1)} all-reduce(f32[1024]{0:T(1024)S(1)} %psum.30), channel_id=1, replica_groups=mesh['seq'=32,'tp'=4,'dp'=2] {'seq'}, use_global_device_ids=true, to_apply=%region_5.0 | all-reduce | flops 1024 | bytes 8192 | tf_op jit(solution)/shard_map/psum | solution.py:13
  541.8 134.2 %all-reduce.6.cloned.1.call-done = f32[1024,128]{0,1:T(8,128)} async-done(((f32[1024,128]{0,1:T(8,128)}), f32[1024,128]{0,1:T(8,128)}) %all-reduce.6.cloned.1.call-update) | async-done | bytes 524304 | tf_op jit(solution)/shard_map/psum | solution.py:13
  678.1 376.1 %reduce-scatter.4.cloned.1.call-done = f32[64,1024]{1,0:T(8,128)} async-done(((f32[4096,1024]{1,0:T(8,128)}), f32[64,1024]{1,0:T(8,128)}) %reduce-scatter.4.cloned.1.call-update) | async-done | bytes 262160
  (49 shorter events, 23.0 us)
Async XLA Ops:
  7.2 38.3 %all-gather.6.cloned.1.call-start = ((), (), s32[]{:S(2)}) async-start(), calls=%async_computation.4 | async-start | bytes 2621440 | tf_op jit(solution)/shard_map/all_gather | solution.py:90
  7.9 150.1 %all-gather.4.cloned.1.call-start = ((), (), s32[]{:S(2)}) async-start(), calls=%async_computation.1 | async-start | bytes 12582912 | tf_op jit(solution)/shard_map/all_gather | solution.py:94
  8.6 451.6 %all-reduce.4.cloned.1.call-start = ((), (), s32[]{:S(2)}) async-start(), calls=%async_computation.2 | async-start | bytes 1048576 | tf_op jit(solution)/shard_map/psum | solution.py:13
  29.0 129.0 %copy-start.1 = (bf16[1,256,1024]{2,1,0:T(8,128)(2,1)S(1)}, bf16[1,256,1024]{2,1,0:T(8,128)(2,1)}, u32[]{:S(2)}) copy-start(bf16[1,256,1024]{2,1,0:T(8,128)(2,1)} %param.9) | copy-start | bytes 1572868
  29.0 129.0 %copy-start.2 = (bf16[1,256,1024]{2,1,0:T(8,128)(2,1)S(1)}, bf16[1,256,1024]{2,1,0:T(8,128)(2,1)}, u32[]{:S(2)}) copy-start(bf16[1,256,1024]{2,1,0:T(8,128)(2,1)} %param.8) | copy-start | bytes 1572868
  29.0 129.0 %copy-start.3 = (bf16[1,256,1024]{2,1,0:T(8,128)(2,1)S(1)}, bf16[1,256,1024]{2,1,0:T(8,128)(2,1)}, u32[]{:S(2)}) copy-start(bf16[1,256,1024]{2,1,0:T(8,128)(2,1)} %param.7) | copy-start | bytes 1572868
  166.3 42.7 %collective-permute-start.1 = (bf16[127,1024]{1,0:T(8,128)(2,1)}, bf16[127,1024]{1,0:T(8,128)(2,1)}, u32[]{:S(2)}, u32[]{:S(2)}) collective-permute-start(bf16[127,1024]{1,0:T(8,128)(2,1)} %slice.121), channel_id=1, source_target_pairs={{8,0},{16,8},{24,16},{32,24},{40,32},{48,40},{56,48},{64,56},{72,6... | collective-permute-start | bytes 780296 | tf_op jit(solution)/shard_map/ppermute | solution.py:23
  206.6 48.4 %collective-permute-start = (bf16[127,1024]{1,0:T(8,128)(2,1)S(1)}, bf16[127,1024]{1,0:T(8,128)(2,1)S(1)}, u32[]{:S(2)}, u32[]{:S(2)}) collective-permute-start(bf16[127,1024]{1,0:T(8,128)(2,1)S(1)} %slice.106), channel_id=1, source_target_pairs={{0,8},{8,16},{16,24},{24,32},{32,40},{40,48},{48,56},{56,64},{64,7... | collective-permute-start | bytes 780296 | tf_op jit(solution)/shard_map/ppermute | solution.py:23
  335.5 11.4 %copy-start = (bf16[16,16,1024]{1,0,2:T(8,128)(2,1)S(1)}, bf16[16,16,1024]{1,0,2:T(8,128)(2,1)}, u32[]{:S(2)}) copy-start(bf16[16,16,1024]{1,0,2:T(8,128)(2,1)} %copy.74) | copy-start | bytes 1572868
  398.0 278.0 %all-reduce.6.cloned.1.call-start = ((), (), s32[]{:S(2)}) async-start(), calls=%async_computation.3 | async-start | bytes 1048576 | tf_op jit(solution)/shard_map/psum | solution.py:13
  445.3 11.1 %copy-start.4 = (f32[1024]{0:T(1024)S(1)}, f32[1024]{0:T(1024)}, u32[]{:S(2)}) copy-start(f32[1024]{0:T(1024)} %param.11) | copy-start | bytes 12292
  460.2 594.0 %reduce-scatter.4.cloned.1.call-start = ((), (), s32[]{:S(2)}) async-start(), calls=%async_computation.5 | async-start | bytes 17039360
Sparse Core Ops, SparseCore 0:
  9.8 35.6 all-gather.5
  47.3 110.6 all-gather.3
  398.2 41.9 all-reduce.3
  460.4 215.6 all-reduce.5
  678.4 375.7 reduce-scatter.3
